TPU v7x, 256 devices: a whole 4x4x8 slice. The times are simulated.
256 devices in a mesh: dp: 64 (over z, x, core), tensor: 4 (over y).
Axes of the slice: x: 4, y: 4, z: 8, core: 2. Of those that a mesh axis runs over, the one named last changes fastest.
Arguments:
- gradients: float32 [64, 128, 3, 28672], P('dp', None, None, 'tensor'), may hold values from -2097152 to 2097152
- token_counts: int32 [64, 3], P('dp'), may hold values from 512 to 6143
- modality: int32 [64], P('dp'), may hold values from 0 to 2
- loss_weight: float32 [3], replicated, may hold values from 0.5 to 2
- master: float32 [128, 3, 28672], P('dp', None, 'tensor'), may hold values from -6 to 6
- moment_one: float32 [128, 3, 28672], P('dp', None, 'tensor'), may hold values from -6 to 6
- moment_two: float32 [128, 3, 28672], P('dp', None, 'tensor'), may hold values from 0.05 to 2
Outputs:
- new_master: float32 [128, 3, 28672], P('dp', None, 'tensor')
- new_moment_one: float32 [128, 3, 28672], P('dp', None, 'tensor')
- new_moment_two: float32 [128, 3, 28672], P('dp', None, 'tensor')
- working_weights: bfloat16 [128, 3, 28672], P(None, None, 'tensor')
Inputs may be any that keep to these rules, and one draw needn't show every extreme that they name: `modality`: 0 is text, 1 image, 2 audio.
All inputs are finite; a program needn't handle non-finite values.
Results may differ from a plain program's by a relative error of at most 0.001.
Values may be sent and summed in bfloat16 or wider, within the bound.
No kernel may reach another device: no remote copies, remote signals or barrier semaphores. Data moves between devices by JAX's collectives and lax.ppermute only.
A program may use at most 128 MiB of HBM per device.

v0:
```python
import jax
import jax.numpy as jnp
from jax import lax
from jax.sharding import Mesh
from jax.sharding import PartitionSpec as P

DP = ("dp_0", "dp_1", "dp_2")
beta_one = 0.9
beta_two = 0.95
bias_one = 1.0 - 0.9**10
bias_two = 1.0 - 0.95**10
epsilon = 1e-08
learn_rate = 0.01
decay_rate = 0.1


def in_order(parts, dim):
    parts = jnp.moveaxis(parts, 0, dim)
    dims = parts.shape
    return parts.reshape(*dims[:dim], dims[dim] * dims[dim + 1], *dims[dim + 2 :])


def all_blocks(value, axes, turns):
    parts = value[None]
    for k in turns:
        parts = lax.all_gather(parts, axes[k], axis=0, tiled=True)
    current = [lax.axis_size(axes[k]) for k in reversed(turns)]
    parts = parts.reshape(*current, *value.shape)
    turned = sorted(range(len(turns)), key=lambda place: turns[len(turns) - 1 - place])
    return parts.transpose(*turned, *range(len(turns), parts.ndim)).reshape(-1, *value.shape)


def gather_axes(value, axes, turns, dim):
    return in_order(all_blocks(value, axes, turns), dim)


def from_everyone(value, axis):
    devices = lax.axis_size(axis)
    return lax.all_to_all(
        jnp.broadcast_to(value[None], (devices, *value.shape)), axis, 0, 0, tiled=True
    )


def taken_together(value, axis):
    return from_everyone(value, axis).sum(axis=0)


def scatter_axes(value, axes, dim):
    if not axes:
        return value
    nearer = lax.psum_scatter(value, axes[0], scatter_dimension=dim, tiled=True)
    return scatter_axes(nearer, axes[1:], dim)


def adam_update(grad_sum, first, second, weights):
    first_new = beta_one * first + (1.0 - beta_one) * grad_sum
    second_new = beta_two * second + (1.0 - beta_two) * grad_sum * grad_sum
    step_size = first_new / bias_one / (jnp.sqrt(second_new / bias_two) + epsilon)
    weights_new = weights - learn_rate * (step_size + decay_rate * weights)
    return (weights_new, first_new, second_new)


def publish(weights_new):
    return gather_axes(weights_new.astype(jnp.bfloat16), DP, (1, 0, 2), 0)


def local(gradients, token_counts, modality, loss_weight, master, moment_one, moment_two):
    totals = taken_together(token_counts[0], DP).astype(jnp.float32)
    ratios = loss_weight / totals
    picked = (lax.iota(jnp.int32, 3) == modality[0]).astype(jnp.float32)
    own_scale = jnp.sum(picked * ratios)
    replica_grad = gradients[0]
    summed = scatter_axes(replica_grad * own_scale, DP, 0)
    weights_new, first_new, second_new = adam_update(summed, moment_one, moment_two, master)
    return (weights_new, first_new, second_new, publish(weights_new))


def solution(mesh):
    torus = Mesh(
        mesh.devices.reshape(8, 4, 2, mesh.shape["tensor"]), ("dp_0", "dp_1", "dp_2", "tensor")
    )
    in_specs = (
        P(DP, None, None, "tensor"),
        P(DP, None),
        P(DP),
        P(),
        P(DP, None, "tensor"),
        P(DP, None, "tensor"),
        P(DP, None, "tensor"),
    )
    out_specs = (
        P(DP, None, "tensor"),
        P(DP, None, "tensor"),
        P(DP, None, "tensor"),
        P(None, None, "tensor"),
    )
    return jax.shard_map(local, mesh=torus, in_specs=in_specs, out_specs=out_specs, check_vma=False)
```

profile of v0, /device:TPU:1, one launch (start us, length us, event | category | flops | bytes accessed | tf_op | source)
XLA Modules:
  0.0 351.3 jit_solution(10869749909884527604)
XLA Ops:
  7.2 1.3 broadcast_in_dim.8
  8.5 13.0 %all-to-all-start = ((s32[64,1,3]{2,1,0:T(1,128)}), s32[64,1,3]{2,1,0:T(1,128)S(1)}, u32[]{:S(2)}, u32[]{:S(2)}) async-start(s32[64,1,3]{2,1,0:T(1,128)} %broadcast_in_dim.8), calls=%async_computation | async-start | bytes 65536 | tf_op jit(solution)/shard_map/all_to_all | solution.py:39
  21.4 0.0 reduce-scatter.4.cloned.1.call-start
  22.1 8.6 %all-to-all-done = s32[64,1,3]{2,1,0:T(1,128)S(1)} async-done(((s32[64,1,3]{2,1,0:T(1,128)}), s32[64,1,3]{2,1,0:T(1,128)S(1)}, u32[]{:S(2)}, u32[]{:S(2)}) %all-to-all-start) | async-done | bytes 800 | tf_op jit(solution)/shard_map/all_to_all | solution.py:39
  30.8 0.1 reduce_sum.18
  30.8 1.3 fusion.1
  32.1 10.2 %multiply_bitcast_fusion = f32[128,3,7168]{2,0,1:T(8,128)} fusion(f32[1,128,3,7168]{3,1,2,0:T(8,128)} %param.7, f32[]{:T(128)} %fusion.1), kind=kLoop, calls=%fused_computation | loop fusion | flops 2752512 | bytes 22020100 | tf_op jit(solution)/shard_map/mul | solution.py:73
  42.3 0.0 copy-start.4
  42.3 0.0 copy-start.3
  42.3 0.0 copy-start
  42.3 0.0 copy-start.1
  42.3 0.0 copy-start.2
  42.3 0.0 reduce-scatter.4.cloned.1.call-update
  42.4 0.0 all-reduce.5.cloned.1.call-start
  42.4 114.5 %reduce-scatter.4.cloned.1.call-done = f32[16,3,7168]{2,0,1:T(8,128)} async-done(((f32[128,3,7168]{2,0,1:T(8,128)}), f32[16,3,7168]{2,0,1:T(8,128)}) %reduce-scatter.4.cloned.1.call-update) | async-done | bytes 1376272 | tf_op jit(solution)/shard_map/reduce_scatter | solution.py:51
  156.9 0.0 all-reduce.5.cloned.1.call-update
  156.9 0.0 all-reduce.7.cloned.1.call-start
  157.0 0.0 copy-done.4
  157.0 0.6 dynamic-slice
  158.2 52.2 %all-reduce.5.cloned.1.call-done = f32[16,3,7168]{2,0,1:T(8,128)} async-done(((f32[16,3,7168]{2,0,1:T(8,128)}), f32[16,3,7168]{2,0,1:T(8,128)}) %all-reduce.5.cloned.1.call-update) | async-done | bytes 1376272
  210.4 1.9 constant_dynamic-slice_fusion
  212.3 0.0 all-reduce.7.cloned.1.call-update
  212.3 0.0 all-gather.4.cloned.1.call-start
  212.4 0.0 copy-done.3
  212.4 0.6 dynamic-slice.2
  213.6 31.2 %all-reduce.7.cloned.1.call-done = f32[4,3,7168]{2,0,1:T(4,128)} async-done(((f32[4,3,7168]{2,0,1:T(4,128)}), f32[4,3,7168]{2,0,1:T(4,128)}) %all-reduce.7.cloned.1.call-update) | async-done | bytes 344080
  244.8 0.0 copy-done
  244.8 0.0 copy-done.1
  244.8 0.0 copy-done.2
  244.8 2.4 fusion.2
  247.2 10.5 %all-gather = bf16[8,3,7168]{2,1,0:T(4,128)(2,1)S(1)} all-gather(bf16[2,3,7168]{2,1,0:T(4,128)(2,1)S(1)} %copy.25), channel_id=2, replica_groups=mesh['dp_0'=8,'dp_1'=4,'dp_2'=2,'tensor'=4] {'dp_1'}, dimensions={0}, use_global_device_ids=true | all-gather | bytes 430080 | tf_op jit(solution)/shard_map/all_gather | solution.py:26
  257.7 1.0 copy.26
  258.8 0.0 all-gather.4.cloned.1.call-update
  258.8 0.0 all-gather.6.cloned.1.call-start
  258.8 43.1 %all-gather.4.cloned.1.call-done = bf16[32,2,3,7168]{3,1,2,0:T(2,128)(2,1)} async-done(((bf16[4,2,3,7168]{3,1,2,0:T(2,128)(2,1)}), bf16[32,2,3,7168]{3,1,2,0:T(2,128)(2,1)}) %all-gather.4.cloned.1.call-update) | async-done | bytes 2752528 | tf_op jit(solution)/shard_map/all_gather | solution.py:26
  301.9 0.0 all-gather.6.cloned.1.call-update
  301.9 24.7 %all-gather.6.cloned.1.call-done = bf16[64,2,3,7168]{3,1,2,0:T(2,128)(2,1)} async-done(((bf16[32,2,3,7168]{3,1,2,0:T(2,128)(2,1)}), bf16[64,2,3,7168]{3,1,2,0:T(2,128)(2,1)}) %all-gather.6.cloned.1.call-update) | async-done | bytes 5505040 | tf_op jit(solution)/shard_map/all_gather | solution.py:26
  326.6 6.4 %copy.27 = bf16[8,4,2,2,3,7168]{5,3,2,1,0,4:T(2,128)(2,1)} copy(bf16[8,4,2,2,3,7168]{5,3,4,1,0,2:T(2,128)(2,1)} %bitcast.13) | data formatting | bytes 11010048 | tf_op jit(solution)/shard_map/transpose | solution.py:30
  333.0 11.8 %reshape_reshape.3 = bf16[128,3,7168]{2,0,1:T(8,128)(2,1)} reshape(bf16[8,4,2,2,3,7168]{5,3,2,1,0,4:T(2,128)(2,1)} %copy.27) | data formatting | bytes 11010048 | tf_op jit(solution)/shard_map/reshape;reshape | solution.py:20
  (1 shorter events, 0.0 us)
Async XLA Ops:
  8.5 22.3 %all-to-all-start = ((s32[64,1,3]{2,1,0:T(1,128)}), s32[64,1,3]{2,1,0:T(1,128)S(1)}, u32[]{:S(2)}, u32[]{:S(2)}) async-start(s32[64,1,3]{2,1,0:T(1,128)} %broadcast_in_dim.8), calls=%async_computation | async-start | bytes 65536 | tf_op jit(solution)/shard_map/all_to_all | solution.py:39
  21.4 135.5 %reduce-scatter.4.cloned.1.call-start = ((), (), s32[]{:S(2)}) async-start(), calls=%async_computation.2 | async-start | bytes 12386304 | tf_op jit(solution)/shard_map/reduce_scatter | solution.py:51
  42.3 114.7 %copy-start.4 = (u32[256]{0:T(256)S(1)}, u32[256]{0:T(256)}, u32[]{:S(2)}) copy-start(u32[256]{0:T(256)} %constant.31) | copy-start | bytes 3076
  42.3 170.0 %copy-start.3 = (u32[256]{0:T(256)S(1)}, u32[256]{0:T(256)}, u32[]{:S(2)}) copy-start(u32[256]{0:T(256)} %constant.35) | copy-start | bytes 3076
  42.3 202.4 %copy-start = (f32[2,3,7168]{2,0,1:T(2,128)S(1)}, f32[2,3,7168]{2,0,1:T(2,128)}, u32[]{:S(2)}) copy-start(f32[2,3,7168]{2,0,1:T(2,128)} %param.11) | copy-start | bytes 516100
  42.3 202.4 %copy-start.1 = (f32[2,3,7168]{2,0,1:T(2,128)S(1)}, f32[2,3,7168]{2,0,1:T(2,128)}, u32[]{:S(2)}) copy-start(f32[2,3,7168]{2,0,1:T(2,128)} %param.12) | copy-start | bytes 516100
  42.3 202.4 %copy-start.2 = (f32[2,3,7168]{2,0,1:T(2,128)S(1)}, f32[2,3,7168]{2,0,1:T(2,128)}, u32[]{:S(2)}) copy-start(f32[2,3,7168]{2,0,1:T(2,128)} %param.13) | copy-start | bytes 516100
  42.4 168.0 %all-reduce.5.cloned.1.call-start = ((), (), s32[]{:S(2)}) async-start(), calls=%async_computation.5 | async-start | bytes 2752512
  156.9 87.8 %all-reduce.7.cloned.1.call-start = ((), (), s32[]{:S(2)}) async-start(), calls=%async_computation.6 | async-start | bytes 688128
  212.3 89.6 %all-gather.4.cloned.1.call-start = ((), (), s32[]{:S(2)}) async-start(), calls=%async_computation.3 | async-start | bytes 3096576 | tf_op jit(solution)/shard_map/all_gather | solution.py:26
  258.8 67.8 %all-gather.6.cloned.1.call-start = ((), (), s32[]{:S(2)}) async-start(), calls=%async_computation.4 | async-start | bytes 8257536 | tf_op jit(solution)/shard_map/all_gather | solution.py:26
Sparse Core Ops, SparseCore 0:
  42.5 114.3 reduce-scatter.3
  159.3 51.0 all-reduce.4
  213.6 31.1 all-reduce.6
  258.9 42.9 all-gather.3
  303.6 23.0 all-gather.5
where the time goes:
time: 352 us; the launch traced here: 351 us
  waiting for transfers between devices  274 us (78%)
  local copies, waits for them, and re-layouts  23.7 us (7%)
  between operations  15.8 us (4%)
  other arithmetic  13.9 us (4%)
  starting transfers between devices  13.2 us (4%)
  blocking collectives  10.5 us (3%)
    reduce_scatter x1, waiting for transfers between devices, scatter_axes(): nearer = lax.psum_scatter(value, axes[0], scatter_dimension=dim, tiled=True)  114 us
    unnamed x7, waiting for transfers between devices  83.4 us
    all_gather x2, waiting for transfers between devices, all_blocks(): parts = lax.all_gather(parts, axes[k], axis=0, tiled=True)  67.7 us
    all_to_all x1, starting transfers between devices, from_everyone(): lax.all_to_all(jnp.broadcast_to(value[None], (devices, *value.shape)), ax...  13 us
    another operation x1, local copies, waits for them, and re-layouts, in_order(): parts.reshape(*dims[:dim], dims[dim] * dims[dim + 1], *dims[dim + 2:])  11.8 us
    all_gather x1, blocking collectives, all_blocks(): parts = lax.all_gather(parts, axes[k], axis=0, tiled=True)  10.5 us
    mul x1, other arithmetic, local(): summed = scatter_axes(replica_grad * own_scale, DP, 0)  10.2 us
    all_to_all x1, waiting for transfers between devices, from_everyone(): lax.all_to_all(jnp.broadcast_to(value[None], (devices, *value.shape)), ax...  8.63 us
  transfers between devices with their start and end apart: 6, of which 6 were waited for; matrix products, arithmetic and copies ran while one was open for 0% of the time, Pallas kernels for 0%

commit v1 on v0

--- a/solution.py
+++ b/solution.py
@@ -23,7 +23,10 @@
 def all_blocks(value, axes, turns):
     parts = value[None]
     for k in turns:
-        parts = lax.all_gather(parts, axes[k], axis=0, tiled=True)
+        work_x = axes[k]
+        t_next = jnp.stack([parts] * lax.axis_size(work_x), 0)
+        reply = lax.all_to_all(t_next, axis_name=work_x, split_axis=0, concat_axis=0)
+        parts = jnp.concatenate(reply, 0)
     current = [lax.axis_size(axes[k]) for k in reversed(turns)]
     parts = parts.reshape(*current, *value.shape)
     turned = sorted(range(len(turns)), key=lambda place: turns[len(turns) - 1 - place])

time: 352 us -> 379 us (1.077)
  blocking collectives: 10.5 us -> 90.8 us
  waiting for transfers between devices: 274 us -> 207 us
  local copies, waits for them, and re-layouts: 23.7 us -> 32.2 us
  other arithmetic: 13.9 us -> 19.9 us
    all_to_all x0 -> x3, blocking collectives: none -> 90.8 us  [all_blocks(): lax.all_to_all(t_next, axis_name=work_x, split_axis=0, concat_axis=0)]
    all_gather x2 -> x0, waiting for transfers between devices: 67.7 us -> none  [all_blocks(): parts = lax.all_gather(parts, axes[k], axis=0, tiled=True)]
    all_gather x1 -> x0, blocking collectives: 10.5 us -> none  [all_blocks(): parts = lax.all_gather(parts, axes[k], axis=0, tiled=True)]
    another operation x0 -> x4, local copies, waits for them, and re-layouts: none -> 9.01 us  [all_blocks(): t_next = jnp.stack([parts] * lax.axis_size(work_x), 0)]
    another operation x0 -> x1, other arithmetic: none -> 5.97 us  [all_blocks(): t_next = jnp.stack([parts] * lax.axis_size(work_x), 0)]
    unnamed x7 -> x5, waiting for transfers between devices: 83.4 us -> 83.4 us
  transfers between devices with their start and end apart: 6 -> 4, of which waited for: 6 -> 4; matrix products, arithmetic and copies ran while one was open for 0% -> 0% of each run, Pallas kernels for 0% -> 0%
where the time goes in v1:
time: 379 us; the launch traced here: 378 us
  waiting for transfers between devices  207 us (55%)
  blocking collectives  90.8 us (24%)
  local copies, waits for them, and re-layouts  32.2 us (8%)
  other arithmetic  19.9 us (5%)
  between operations  15.8 us (4%)
  starting transfers between devices  13.1 us (3%)
    reduce_scatter x1, waiting for transfers between devices, scatter_axes(): nearer = lax.psum_scatter(value, axes[0], scatter_dimension=dim, tiled=True)  114 us
    all_to_all x3, blocking collectives, all_blocks(): lax.all_to_all(t_next, axis_name=work_x, split_axis=0, concat_axis=0)  90.8 us
    unnamed x5, waiting for transfers between devices  83.4 us
    all_to_all x1, starting transfers between devices, from_everyone(): lax.all_to_all(jnp.broadcast_to(value[None], (devices, *value.shape)), ax...  13 us
    another operation x1, local copies, waits for them, and re-layouts, in_order(): parts.reshape(*dims[:dim], dims[dim] * dims[dim + 1], *dims[dim + 2:])  11.8 us
    mul x1, other arithmetic, local(): summed = scatter_axes(replica_grad * own_scale, DP, 0)  10.2 us
    another operation x4, local copies, waits for them, and re-layouts, all_blocks(): t_next = jnp.stack([parts] * lax.axis_size(work_x), 0)  9.01 us
    all_to_all x1, waiting for transfers between devices, from_everyone(): lax.all_to_all(jnp.broadcast_to(value[None], (devices, *value.shape)), ax...  8.63 us
  transfers between devices with their start and end apart: 4, of which 4 were waited for; matrix products, arithmetic and copies ran while one was open for 0% of the time, Pallas kernels for 0%

profile of v1, /device:TPU:1, one launch (start us, length us, event | category | flops | bytes accessed | tf_op | source)
XLA Modules:
  0.0 378.3 jit_solution(13479106348608060170)
XLA Ops:
  7.2 1.3 broadcast_in_dim.2
  8.5 13.0 %all-to-all-start = ((s32[64,1,3]{2,1,0:T(1,128)}), s32[64,1,3]{2,1,0:T(1,128)S(1)}, u32[]{:S(2)}, u32[]{:S(2)}) async-start(s32[64,1,3]{2,1,0:T(1,128)} %broadcast_in_dim.2), calls=%async_computation | async-start | bytes 65536 | tf_op jit(solution)/shard_map/all_to_all | solution.py:42
  21.4 0.0 reduce-scatter.4.cloned.1.call-start
  22.1 8.6 %all-to-all-done = s32[64,1,3]{2,1,0:T(1,128)S(1)} async-done(((s32[64,1,3]{2,1,0:T(1,128)}), s32[64,1,3]{2,1,0:T(1,128)S(1)}, u32[]{:S(2)}, u32[]{:S(2)}) %all-to-all-start) | async-done | bytes 800 | tf_op jit(solution)/shard_map/all_to_all | solution.py:42
  30.8 0.1 reduce_sum.18
  30.8 1.3 fusion.1
  32.1 10.2 %multiply_bitcast_fusion = f32[128,3,7168]{2,0,1:T(8,128)} fusion(f32[1,128,3,7168]{3,1,2,0:T(8,128)} %param.7, f32[]{:T(128)} %fusion.1), kind=kLoop, calls=%fused_computation | loop fusion | flops 2752512 | bytes 22020100 | tf_op jit(solution)/shard_map/mul | solution.py:76
  42.3 0.0 copy-start.4
  42.3 0.0 copy-start.3
  42.3 0.0 copy-start
  42.3 0.0 copy-start.1
  42.3 0.0 copy-start.2
  42.3 0.0 reduce-scatter.4.cloned.1.call-update
  42.4 0.0 all-reduce.5.cloned.1.call-start
  42.4 114.5 %reduce-scatter.4.cloned.1.call-done = f32[16,3,7168]{2,0,1:T(8,128)} async-done(((f32[128,3,7168]{2,0,1:T(8,128)}), f32[16,3,7168]{2,0,1:T(8,128)}) %reduce-scatter.4.cloned.1.call-update) | async-done | bytes 1376272 | tf_op jit(solution)/shard_map/reduce_scatter | solution.py:54
  156.9 0.0 all-reduce.5.cloned.1.call-update
  156.9 0.0 all-reduce.7.cloned.1.call-start
  157.0 0.0 copy-done.4
  157.0 0.6 dynamic-slice
  158.2 52.2 %all-reduce.5.cloned.1.call-done = f32[16,3,7168]{2,0,1:T(8,128)} async-done(((f32[16,3,7168]{2,0,1:T(8,128)}), f32[16,3,7168]{2,0,1:T(8,128)}) %all-reduce.5.cloned.1.call-update) | async-done | bytes 1376272
  210.4 1.9 constant_dynamic-slice_fusion
  212.3 0.0 all-reduce.7.cloned.1.call-update
  212.3 0.0 copy-done.3
  212.3 0.6 dynamic-slice.2
  213.6 31.2 %all-reduce.7.cloned.1.call-done = f32[4,3,7168]{2,0,1:T(4,128)} async-done(((f32[4,3,7168]{2,0,1:T(4,128)}), f32[4,3,7168]{2,0,1:T(4,128)}) %all-reduce.7.cloned.1.call-update) | async-done | bytes 344080
  244.8 0.0 copy-done
  244.8 0.0 copy-done.1
  244.8 0.0 copy-done.2
  244.8 2.4 fusion.2
  247.1 0.2 stack.9
  247.3 10.3 %all_to_all.21 = bf16[4,1,2,3,7168]{4,2,3,1,0:T(2,128)(2,1)S(1)} all-to-all(bf16[4,1,2,3,7168]{4,2,3,1,0:T(2,128)(2,1)S(1)} %stack.9), channel_id=1, replica_groups=mesh['dp_0'=8,'dp_1'=4,'dp_2'=2,'tensor'=4] {'dp_1'}, dimensions={0} | all-to-all | bytes 688128 | tf_op jit(solution)/shard_map/all_to_all | solution.py:28
  257.7 0.2 copy.27
  257.9 2.5 stack.10
  260.4 69.1 %all_to_all.22 = bf16[8,4,2,3,7168]{4,2,1,3,0:T(2,128)(2,1)S(1)} all-to-all(bf16[8,4,2,3,7168]{4,2,1,3,0:T(2,128)(2,1)S(1)} %stack.10), channel_id=1, replica_groups=mesh['dp_0'=8,'dp_1'=4,'dp_2'=2,'tensor'=4] {'dp_0'}, dimensions={0} | all-to-all | bytes 5505024 | tf_op jit(solution)/shard_map/all_to_all | solution.py:28
  329.5 2.1 copy.28
  331.6 6.0 %pad_maximum_fusion = bf16[2,32,2,3,7168]{4,2,3,1,0:T(2,128)(2,1)S(1)} fusion(bf16[1,32,2,3,7168]{4,2,3,1,0:T(2,128)(2,1)S(1)} %bitcast.15), kind=kLoop, calls=%fused_computation.1 | loop fusion | flops 2752512 | bytes 8257536 | tf_op jit(solution)/shard_map/stack | solution.py:27
  337.6 6.1 %copy.29 = bf16[2,32,2,3,7168]{4,2,1,3,0:T(2,128)(2,1)S(1)} copy(bf16[2,32,2,3,7168]{4,2,3,1,0:T(2,128)(2,1)S(1)} %pad_maximum_fusion) | data formatting | bytes 11010048 | tf_op jit(solution)/shard_map/stack | solution.py:27
  343.8 11.4 %all_to_all.23 = bf16[2,32,2,3,7168]{4,2,1,3,0:T(2,128)(2,1)S(1)} all-to-all(bf16[2,32,2,3,7168]{4,2,1,3,0:T(2,128)(2,1)S(1)} %copy.29), channel_id=1, replica_groups=mesh['dp_0'=8,'dp_1'=4,'dp_2'=2,'tensor'=4] {'dp_2'}, dimensions={0} | all-to-all | bytes 11010048 | tf_op jit(solution)/shard_map/all_to_all | solution.py:28
  355.1 4.9 %copy.30 = bf16[8,4,2,2,3,7168]{5,3,2,1,0,4:T(2,128)(2,1)} copy(bf16[8,4,2,2,3,7168]{5,3,1,0,4,2:T(2,128)(2,1)S(1)} %bitcast.14) | data formatting | bytes 11010048 | tf_op jit(solution)/shard_map/transpose | solution.py:33
  360.0 11.8 %reshape_reshape.7 = bf16[128,3,7168]{2,0,1:T(8,128)(2,1)} reshape(bf16[8,4,2,2,3,7168]{5,3,2,1,0,4:T(2,128)(2,1)} %copy.30) | data formatting | bytes 11010048 | tf_op jit(solution)/shard_map/reshape;reshape | solution.py:20
Async XLA Ops:
  8.5 22.3 %all-to-all-start = ((s32[64,1,3]{2,1,0:T(1,128)}), s32[64,1,3]{2,1,0:T(1,128)S(1)}, u32[]{:S(2)}, u32[]{:S(2)}) async-start(s32[64,1,3]{2,1,0:T(1,128)} %broadcast_in_dim.2), calls=%async_computation | async-start | bytes 65536 | tf_op jit(solution)/shard_map/all_to_all | solution.py:42
  21.4 135.5 %reduce-scatter.4.cloned.1.call-start = ((), (), s32[]{:S(2)}) async-start(), calls=%async_computation.5 | async-start | bytes 12386304 | tf_op jit(solution)/shard_map/reduce_scatter | solution.py:54
  42.3 114.7 %copy-start.4 = (u32[256]{0:T(256)S(1)}, u32[256]{0:T(256)}, u32[]{:S(2)}) copy-start(u32[256]{0:T(256)} %constant.31) | copy-start | bytes 3076
  42.3 170.0 %copy-start.3 = (u32[256]{0:T(256)S(1)}, u32[256]{0:T(256)}, u32[]{:S(2)}) copy-start(u32[256]{0:T(256)} %constant.35) | copy-start | bytes 3076
  42.3 202.4 %copy-start = (f32[2,3,7168]{2,0,1:T(2,128)S(1)}, f32[2,3,7168]{2,0,1:T(2,128)}, u32[]{:S(2)}) copy-start(f32[2,3,7168]{2,0,1:T(2,128)} %param.11) | copy-start | bytes 516100
  42.3 202.4 %copy-start.1 = (f32[2,3,7168]{2,0,1:T(2,128)S(1)}, f32[2,3,7168]{2,0,1:T(2,128)}, u32[]{:S(2)}) copy-start(f32[2,3,7168]{2,0,1:T(2,128)} %param.12) | copy-start | bytes 516100
  42.3 202.4 %copy-start.2 = (f32[2,3,7168]{2,0,1:T(2,128)S(1)}, f32[2,3,7168]{2,0,1:T(2,128)}, u32[]{:S(2)}) copy-start(f32[2,3,7168]{2,0,1:T(2,128)} %param.13) | copy-start | bytes 516100
  42.4 168.0 %all-reduce.5.cloned.1.call-start = ((), (), s32[]{:S(2)}) async-start(), calls=%async_computation.6 | async-start | bytes 2752512
  156.9 87.8 %all-reduce.7.cloned.1.call-start = ((), (), s32[]{:S(2)}) async-start(), calls=%async_computation.7 | async-start | bytes 688128
Sparse Core Ops, SparseCore 0:
  42.5 114.3 reduce-scatter.3
  159.3 51.0 all-reduce.4
  213.6 31.1 all-reduce.6
